TPU v7x, 256 devices: a whole 4x4x8 slice. The times are simulated.
256 devices in a mesh: space: 64 (over x, y, z_lo), load: 4 (over z_hi, core).
Axes of the slice: x: 4, y: 4, z: 8 (z_hi: 2, z_lo: 4; z = z_hi * 4 + z_lo), core: 2. Of those that a mesh axis runs over, the one named last changes fastest.
Arguments:
- load_force: float32 [4, 3, 512, 16, 256], P('load', None, 'space'), may hold values from -6 to 6
- stiffness: float32 [512, 16, 256], P('space'), may hold values from 0.5 to 4
- material: int32 [64, 2], P('space'), may hold values from 0 to 2
- face_src: int32 [64, 64, 256], P('space'), may hold values from 0 to 32767
- face_count: int32 [64, 64], P('space'), may hold values from 0 to 256, as said below
- face_dst: int32 [64, 64, 256], P('space'), may hold values from 0 to 4095
Outputs:
- displacement: float32 [4, 3, 512, 16, 256], P('load', None, 'space')
- sensitivity: float32 [3, 512, 16, 256], P(None, 'space', 'load')
Inputs may be any that keep to these rules, and one draw needn't show every extreme that they name: face_count[s, o] counts the live first slots from slab s to owner o; in every row one owner gets all 256.
All inputs are finite; a program needn't handle non-finite values.
Results may differ from a plain program's by a relative error of at most 0.0001.
Values sent between devices are 32-bit elements; how exact they have to be, the bound alone decides.
No kernel may reach another device: no remote copies, remote signals or barrier semaphores. Data moves between devices by JAX's collectives and lax.ppermute only.
A program may use at most 192 MiB of HBM per device.

v0:
```python
import jax
import jax.numpy as jnp
from jax import lax
from jax.sharding import PartitionSpec as P

NY = 16
BY = 8
SLOTS = 256
FINE_STEPS = 3
COARSE_STEPS = 4
UPPER_EDGE = 2.1
LOWER_EDGE = 0.15
COUPLING = 0.1
MODULI = (1.0, 0.55, 0.25)


def extended(block, sides, width):
    for axis, dim in sides:
        count = lax.axis_size(axis)
        forward = [(i, i + 1) for i in range(count - 1)]
        backward = [(target, source) for source, target in forward]
        low = lax.ppermute(
            lax.slice_in_dim(block, block.shape[dim] - width, None, axis=dim), axis, forward
        )
        high = lax.ppermute(lax.slice_in_dim(block, 0, width, axis=dim), axis, backward)
        block = jnp.concatenate([low, block, high], axis=dim)
    return block


def neighbour_list():
    entries = []
    for shift_x in (-1, 0, 1):
        for shift_y in (-1, 0, 1):
            for shift_z in (-1, 0, 1):
                reach_len = abs(shift_x) + abs(shift_y) + abs(shift_z)
                if reach_len > 0:
                    entries.append(
                        (shift_x, shift_y, shift_z, (1.0, 0.5, 0.25)[reach_len - 1] / 14.0)
                    )
    return entries


def window(padded, shift_x, shift_y, shift_z, inner_shape):
    size_x, size_y, size_z = inner_shape
    return padded[
        :,
        1 + shift_x : 1 + shift_x + size_x,
        1 + shift_y : 1 + shift_y + size_y,
        1 + shift_z : 1 + shift_z + size_z,
    ]


def operate(padded_field, padded_coef):
    inner_shape = (padded_field.shape[1] - 2, padded_field.shape[2] - 2, padded_field.shape[3] - 2)
    centre = window(padded_field, 0, 0, 0, inner_shape)
    coef_mid = window(padded_coef, 0, 0, 0, inner_shape)
    result = jnp.zeros_like(centre)
    for shift_x, shift_y, shift_z, weight in neighbour_list():
        face_coef = 0.5 * (coef_mid + window(padded_coef, shift_x, shift_y, shift_z, inner_shape))
        result = result + weight * face_coef * (
            centre - window(padded_field, shift_x, shift_y, shift_z, inner_shape)
        )
    pieces = []
    for component in range(3):
        mixed_term = jnp.zeros_like(coef_mid[0])
        for partner in range(3):
            if partner != component:
                for sign_a in (1, -1):
                    for sign_b in (1, -1):
                        offset = [0, 0, 0]
                        offset[component] += sign_a
                        offset[partner] += sign_b
                        mixed_term = (
                            mixed_term
                            + 0.25
                            * sign_a
                            * sign_b
                            * window(
                                padded_field[partner : partner + 1],
                                offset[0],
                                offset[1],
                                offset[2],
                                inner_shape,
                            )[0]
                        )
        pieces.append(result[component] - COUPLING * coef_mid[0] * mixed_term)
    return jnp.stack(pieces)


def diagonal_of(padded_coef):
    inner_shape = (padded_coef.shape[1] - 2, padded_coef.shape[2] - 2, padded_coef.shape[3] - 2)
    coef_mid = window(padded_coef, 0, 0, 0, inner_shape)
    total_sum = jnp.zeros_like(coef_mid)
    for shift_x, shift_y, shift_z, weight in neighbour_list():
        total_sum = total_sum + weight * 0.5 * (
            coef_mid + window(padded_coef, shift_x, shift_y, shift_z, inner_shape)
        )
    return total_sum


def pad_sides(grid_field):
    return jnp.pad(grid_field, ((0, 0), (0, 0), (1, 1), (1, 1)))


def chebyshev(source, padded_coef, diagonal, sweep_count, widen):
    midpoint = (UPPER_EDGE + LOWER_EDGE) / 2.0
    halfwidth = (UPPER_EDGE - LOWER_EDGE) / 2.0
    spread_ratio = midpoint / halfwidth
    rho_old = 1.0 / spread_ratio
    update = source / (midpoint * diagonal)
    solution = update
    for sweep_idx in range(1, sweep_count):
        residual = source - operate(widen(solution), padded_coef)
        rho_new = 1.0 / (2.0 * spread_ratio - rho_old)
        update = rho_new * rho_old * update + 2.0 * rho_new / halfwidth * residual / diagonal
        solution = solution + update
        rho_old = rho_new
    return solution


def coarsen(grid_field):
    comps, size_x, size_y, size_z = grid_field.shape
    return grid_field.reshape(comps, size_x // 2, 2, size_y // 2, 2, size_z // 2, 2).mean(
        axis=(2, 4, 6)
    )


def refine(grid_field):
    return jnp.repeat(jnp.repeat(jnp.repeat(grid_field, 2, axis=1), 2, axis=2), 2, axis=3)


def modulus_rows(material, brick_rows):
    onehot = (material[..., None] == jnp.arange(len(MODULI), dtype=jnp.int32)).astype(jnp.float32)
    values = jnp.sum(onehot * jnp.array(MODULI, jnp.float32), axis=-1)
    return jnp.repeat(values, brick_rows, axis=-1)


def widen_fine(grid_field):
    planes = extended(grid_field, (("space", 1),), 1)
    return pad_sides(planes)


def body(load_force, stiffness, material, face_src, face_count, face_dst):
    own_cells = modulus_rows(material, BY)[0][None, :, None]
    coef = stiffness * own_cells
    padded_coef = widen_fine(coef[None])
    diag_fine = diagonal_of(padded_coef)
    coarse_coef = coarsen(coef[None])

    def widen_coarse(grid_field):
        planes = extended(grid_field, (("space", 1),), 1)
        return pad_sides(planes)

    padded_coarse = widen_coarse(coarse_coef)
    diag_coarse = diagonal_of(padded_coarse)
    live_mask = (jnp.arange(SLOTS, dtype=jnp.int32)[None, :] < face_count[0][:, None]).astype(
        jnp.float32
    )
    source = load_force[0]
    smooth = chebyshev(source, padded_coef, diag_fine, FINE_STEPS, widen_fine)
    smooth, residual = (smooth, source - operate(widen_fine(smooth), padded_coef))
    coarse_source = 4.0 * coarsen(residual)
    picked = residual.reshape(3, -1)[:, face_src[0]] * live_mask[None]
    arrived = lax.all_to_all(picked, "space", split_axis=1, concat_axis=1, tiled=True)
    coarse_source = (
        coarse_source.reshape(3, -1).at[:, face_dst[0]].add(arrived).reshape(coarse_source.shape)
    )
    displaced = smooth + refine(
        chebyshev(coarse_source, padded_coarse, diag_coarse, COARSE_STEPS, widen_coarse)
    )
    image = operate(widen_fine(displaced), padded_coef)
    energy = jnp.sum(displaced * image, axis=0)
    outputs = [displaced]
    rows_part = NY // lax.axis_size("load")
    start_row = lax.axis_index("load") * rows_part
    total_sum = lax.psum(energy, "load")
    energy_part = lax.dynamic_slice_in_dim(total_sum, start_row, rows_part, 1)
    own_part = lax.dynamic_slice_in_dim(own_cells, start_row, rows_part, 1)[None]
    moduli = jnp.array(MODULI, jnp.float32)[:, None, None, None]
    sensitivity = (moduli - own_part) / own_part * energy_part[None]
    return (jnp.stack(outputs), sensitivity)


def solution(mesh):
    return jax.shard_map(
        body,
        mesh=mesh,
        in_specs=(
            P("load", None, "space", None, None),
            P("space", None, None),
            P("space", None),
            P("space", None, None),
            P("space", None),
            P("space", None, None),
        ),
        out_specs=(P("load", None, "space", None, None), P(None, "space", "load", None)),
        check_vma=False,
    )
```

profile of v0, /device:TPU:1, one launch (start us, length us, event | category | flops | bytes accessed | tf_op | source)
XLA Modules:
  0.0 533.6 jit_solution(4295424980780647665)
XLA Ops:
  10.5 5.0 collective-permute-start
  16.5 9.8 %reshape_broadcast_in_dim.3 = f32[4,2,8,2,128,2]{5,4,3,2,1,0:T(8,128)} reshape(f32[8,16,256]{2,1,0:T(8,128)S(1)} %broadcast_multiply_fusion.1) | data formatting | bytes 262144 | tf_op jit(solution)/shard_map/reshape;broadcast_in_dim | solution.py:123
  26.3 4.1 reduce_sum.38
  31.7 4.2 collective-permute-start.8
  37.3 26.5 %squeeze.11 = f32[3,4,2,8,2,128,2]{6,5,4,3,2,1,0:T(8,128)} reshape(f32[1,3,8,16,256]{4,3,2,1,0:T(8,128)S(1)} %copy-done) | data formatting | bytes 786432 | tf_op jit(solution)/shard_map/squeeze | solution.py:159
  63.9 8.6 %copy.310 = f32[1,3,8,16,256]{1,4,3,2,0:T(8,128)} copy(f32[1,3,8,16,256]{4,3,2,1,0:T(8,128)S(1)} %copy-done) | data formatting | bytes 786432 | tf_op args[0]
  76.2 4.2 collective-permute-start.2
  81.9 2.0 fusion.164
  86.1 6.7 %collective-permute-start.4 = (f32[3,1,16,256]{3,2,1,0:T(8,128)S(1)}, f32[3,1,16,256]{3,2,1,0:T(8,128)S(1)}, u32[]{:S(2)}, u32[]{:S(2)}) collective-permute-start(f32[3,1,16,256]{3,2,1,0:T(8,128)S(1)} %get-tuple-element.56), channel_id=1, source_target_pairs={{0,4},{4,8},{8,12},{12,16},{16,20},{20,24},{24,28},{28,32},{32,36}... | collective-permute-start | bytes 147464 | tf_op jit(solution)/shard_map/ppermute | solution.py:22
  94.3 2.0 fusion.111
  98.7 6.9 %collective-permute-start.6 = (f32[3,1,16,256]{3,2,1,0:T(8,128)S(1)}, f32[3,1,16,256]{3,2,1,0:T(8,128)S(1)}, u32[]{:S(2)}, u32[]{:S(2)}) collective-permute-start(f32[3,1,16,256]{3,2,1,0:T(8,128)S(1)} %get-tuple-element.54), channel_id=1, source_target_pairs={{0,4},{4,8},{8,12},{12,16},{16,20},{20,24},{24,28},{28,32},{32,36}... | collective-permute-start | bytes 147464 | tf_op jit(solution)/shard_map/ppermute | solution.py:22
  107.2 2.0 fusion.58
  109.9 9.7 %stack.91 = f32[1,4,2,8,2,128,2]{6,5,4,3,2,1,0:T(8,128)} reshape(f32[1,8,16,256]{3,2,1,0:T(8,128)S(1)} %fusion.270) | data formatting | bytes 262144 | tf_op jit(solution)/shard_map/stack | solution.py:87
  119.6 9.7 %stack.90 = f32[1,4,2,8,2,128,2]{6,5,4,3,2,1,0:T(8,128)} reshape(f32[1,8,16,256]{3,2,1,0:T(8,128)S(1)} %get-tuple-element.23) | data formatting | bytes 262144 | tf_op jit(solution)/shard_map/stack | solution.py:87
  129.4 9.7 %stack.89 = f32[1,4,2,8,2,128,2]{6,5,4,3,2,1,0:T(8,128)} reshape(f32[1,8,16,256]{3,2,1,0:T(8,128)S(1)} %get-tuple-element.22) | data formatting | bytes 262144 | tf_op jit(solution)/shard_map/stack | solution.py:87
  139.9 8.6 %copy.311 = f32[3,32768]{0,1:T(8,128)} copy(f32[3,32768]{1,0:T(4,128)S(1)} %pad_maximum_fusion) | data formatting | bytes 786432 | tf_op jit(solution)/shard_map/stack | solution.py:87
  148.5 17.8 %bitcast_subtract_fusion = f32[3,32768]{0,1:T(8,128)} fusion(f32[3,32768]{0,1:T(8,128)} %copy.311, f32[1,3,8,16,256]{1,4,3,2,0:T(8,128)} %copy.310), kind=kLoop, calls=%fused_computation.4 | loop fusion | flops 98304 | bytes 1179648 | tf_op jit(solution)/shard_map/sub | solution.py:161
  166.3 60.5 %gather_fusion = f32[16384,3]{1,0:T(8,128)} fusion(f32[3,32768]{0,1:T(8,128)} %bitcast_subtract_fusion, s32[16384]{0:T(1024)S(1)} %copy-done.77), kind=kCustom, calls=%fused_computation | custom fusion | bytes 458752 | tf_op jit(solution)/shard_map/gather | solution.py:163
  226.8 5.4 %copy.312 = f32[64,256,3]{1,2,0:T(4,128)S(1)} copy(f32[64,256,3]{2,1,0:T(8,128)} %bitcast.288) | data formatting | bytes 393216 | tf_op jit(solution)/shard_map/gather | solution.py:163
  233.0 30.9 %all-to-all-start = ((f32[3,64,256]{2,0,1:T(4,128)}), f32[3,64,256]{2,0,1:T(4,128)S(1)}, u32[]{:S(2)}, u32[]{:S(2)}) async-start(f32[3,64,256]{2,0,1:T(4,128)} %multiply_bitcast_fusion), calls=%async_computation | async-start | bytes 524288 | tf_op jit(solution)/shard_map/all_to_all | solution.py:164
  263.9 16.1 %fusion = f32[3,4,8,128]{3,2,1,0:T(8,128)S(1)} fusion(f32[3,4,2,8,2,128,2]{6,5,4,3,2,1,0:T(8,128)} %squeeze.11, f32[1,4,2,8,2,128,2]{6,5,4,3,2,1,0:T(8,128)} %stack.91, f32[1,4,2,8,2,128,2]{6,5,4,3,2,1,0:T(8,128)} %stack.90, f32[1,4,2,8,2,128,2]{6,5,4,3,2,1,0:T(8,128)} %stack.89), kind=kLoop, calls=%fused_computation.3 | loop fusion | flops 380928 | bytes 835584 | tf_op jit(solution)/shard_map/reduce_sum | solution.py:123
  280.7 5.1 copy.313
  285.8 88.6 %scatter_fusion = f32[3,4096]{0,1:T(8,128)S(1)} fusion(f32[3,4096]{0,1:T(8,128)S(1)} %bitcast.286, s32[16384]{0:T(1024)S(1)} %bitcast.312, f32[16384,3]{1,0:T(8,128)} %copy.313), kind=kCustom, calls=%fused_computation.1 | custom fusion | flops 49152 | bytes 655360 | tf_op jit(solution)/shard_map/scatter-add | solution.py:166
  376.6 4.0 collective-permute-start.10
  383.8 4.2 collective-permute-start.12
  390.9 4.2 collective-permute-start.14
  396.7 1.6 copy.319
  400.0 1.8 copy.321
  406.1 5.8 %collective-permute-start.16 = (f32[3,1,16,256]{3,2,1,0:T(8,128)}, f32[3,1,16,256]{3,2,1,0:T(8,128)}, u32[]{:S(2)}, u32[]{:S(2)}) collective-permute-start(f32[3,1,16,256]{3,2,1,0:T(8,128)} %get-tuple-element.52), channel_id=1, source_target_pairs={{0,4},{4,8},{8,12},{12,16},{16,20},{20,24},{24,28},{28,32},{32,36}... | collective-permute-start | bytes 147464 | tf_op jit(solution)/shard_map/ppermute | solution.py:22
  411.9 1.8 copy.320
  415.5 3.3 fusion.5
  422.9 101.1 %all-reduce.11.cloned.1.call-done = f32[8,16,256]{1,0,2:T(8,128)} async-done(((f32[8,16,256]{1,0,2:T(8,128)}), f32[8,16,256]{1,0,2:T(8,128)}) %all-reduce.11.cloned.1.call-update) | async-done | bytes 131088 | tf_op jit(solution)/shard_map/psum | solution.py:176
  (301 shorter events, 45.7 us)
Async XLA Ops:
  8.2 75.9 %copy-start.79 = (f32[16]{0:T(128)}, f32[16]{0:T(128)S(1)}, u32[]{:S(2)}) copy-start(f32[16]{0:T(128)S(1)} %broadcast_in_dim.30) | copy-start | bytes 196
  9.2 64.1 %collective-permute-start.1 = (f32[1,1,16,256]{3,2,1,0:T(8,128)S(1)}, f32[1,1,16,256]{3,2,1,0:T(8,128)S(1)}, u32[]{:S(2)}, u32[]{:S(2)}) collective-permute-start(f32[1,1,16,256]{3,2,1,0:T(8,128)S(1)} %get-tuple-element.69), channel_id=1, source_target_pairs={{4,0},{8,4},{12,8},{16,12},{20,16},{24,20},{28,24},{32,28},{36,32}... | collective-permute-start | bytes 49160 | tf_op jit(solution)/shard_map/ppermute | solution.py:25
  10.5 62.8 %collective-permute-start = (f32[1,1,16,256]{3,2,1,0:T(8,128)S(1)}, f32[1,1,16,256]{3,2,1,0:T(8,128)S(1)}, u32[]{:S(2)}, u32[]{:S(2)}) collective-permute-start(f32[1,1,16,256]{3,2,1,0:T(8,128)S(1)} %get-tuple-element.68), channel_id=1, source_target_pairs={{0,4},{4,8},{8,12},{12,16},{16,20},{20,24},{24,28},{28,32},{32,36}... | collective-permute-start | bytes 49160 | tf_op jit(solution)/shard_map/ppermute | solution.py:22
  30.4 42.7 %collective-permute-start.9 = (f32[1,1,8,128]{3,2,1,0:T(8,128)S(1)}, f32[1,1,8,128]{3,2,1,0:T(8,128)S(1)}, u32[]{:S(2)}, u32[]{:S(2)}) collective-permute-start(f32[1,1,8,128]{3,2,1,0:T(8,128)S(1)} %get-tuple-element.103), channel_id=1, source_target_pairs={{4,0},{8,4},{12,8},{16,12},{20,16},{24,20},{28,24},{32,28},{36,32}... | collective-permute-start | bytes 12296 | tf_op jit(solution)/shard_map/ppermute | solution.py:25
  31.7 41.4 %collective-permute-start.8 = (f32[1,1,8,128]{3,2,1,0:T(8,128)S(1)}, f32[1,1,8,128]{3,2,1,0:T(8,128)S(1)}, u32[]{:S(2)}, u32[]{:S(2)}) collective-permute-start(f32[1,1,8,128]{3,2,1,0:T(8,128)S(1)} %get-tuple-element.102), channel_id=1, source_target_pairs={{0,4},{4,8},{8,12},{12,16},{16,20},{20,24},{24,28},{28,32},{32,36}... | collective-permute-start | bytes 12296 | tf_op jit(solution)/shard_map/ppermute | solution.py:22
  74.0 32.9 %copy-start.15 = (f32[8,16,256]{2,1,0:T(8,128)}, f32[8,16,256]{2,1,0:T(8,128)S(1)}, u32[]{:S(2)}) copy-start(f32[8,16,256]{2,1,0:T(8,128)S(1)} %get-tuple-element.28) | copy-start | bytes 393220
  74.0 32.9 %copy-start.17 = (f32[8,16,256]{2,1,0:T(8,128)}, f32[8,16,256]{2,1,0:T(8,128)S(1)}, u32[]{:S(2)}) copy-start(f32[8,16,256]{2,1,0:T(8,128)S(1)} %get-tuple-element.29) | copy-start | bytes 393220
  74.0 32.9 %copy-start.19 = (f32[8,16,256]{2,1,0:T(8,128)}, f32[8,16,256]{2,1,0:T(8,128)S(1)}, u32[]{:S(2)}) copy-start(f32[8,16,256]{2,1,0:T(8,128)S(1)} %get-tuple-element.30) | copy-start | bytes 393220
  74.0 32.9 %copy-start.21 = (f32[8,16,256]{2,1,0:T(8,128)}, f32[8,16,256]{2,1,0:T(8,128)S(1)}, u32[]{:S(2)}) copy-start(f32[8,16,256]{2,1,0:T(8,128)S(1)} %get-tuple-element.31) | copy-start | bytes 393220
  74.0 32.9 %copy-start.23 = (f32[8,16,256]{2,1,0:T(8,128)}, f32[8,16,256]{2,1,0:T(8,128)S(1)}, u32[]{:S(2)}) copy-start(f32[8,16,256]{2,1,0:T(8,128)S(1)} %get-tuple-element.32) | copy-start | bytes 393220
  74.1 32.9 %copy-start.25 = (f32[8,16,256]{2,1,0:T(8,128)}, f32[8,16,256]{2,1,0:T(8,128)S(1)}, u32[]{:S(2)}) copy-start(f32[8,16,256]{2,1,0:T(8,128)S(1)} %get-tuple-element.33) | copy-start | bytes 393220
  74.1 32.9 %copy-start.27 = (f32[8,16,256]{2,1,0:T(8,128)}, f32[8,16,256]{2,1,0:T(8,128)S(1)}, u32[]{:S(2)}) copy-start(f32[8,16,256]{2,1,0:T(8,128)S(1)} %get-tuple-element.34) | copy-start | bytes 393220
  74.1 32.9 %copy-start.29 = (f32[8,16,256]{2,1,0:T(8,128)}, f32[8,16,256]{2,1,0:T(8,128)S(1)}, u32[]{:S(2)}) copy-start(f32[8,16,256]{2,1,0:T(8,128)S(1)} %get-tuple-element.35) | copy-start | bytes 393220
  74.1 32.9 %copy-start.31 = (f32[8,16,256]{2,1,0:T(8,128)}, f32[8,16,256]{2,1,0:T(8,128)S(1)}, u32[]{:S(2)}) copy-start(f32[8,16,256]{2,1,0:T(8,128)S(1)} %get-tuple-element.36) | copy-start | bytes 393220
  74.1 32.9 %copy-start.33 = (f32[8,16,256]{2,1,0:T(8,128)}, f32[8,16,256]{2,1,0:T(8,128)S(1)}, u32[]{:S(2)}) copy-start(f32[8,16,256]{2,1,0:T(8,128)S(1)} %get-tuple-element.37) | copy-start | bytes 393220
  74.1 32.9 %copy-start.34 = (f32[8,16,256]{2,1,0:T(8,128)}, f32[8,16,256]{2,1,0:T(8,128)S(1)}, u32[]{:S(2)}) copy-start(f32[8,16,256]{2,1,0:T(8,128)S(1)} %get-tuple-element.38) | copy-start | bytes 393220
  74.9 5.8 %collective-permute-start.3 = (f32[3,1,16,256]{3,2,1,0:T(8,128)S(1)}, f32[3,1,16,256]{3,2,1,0:T(8,128)S(1)}, u32[]{:S(2)}, u32[]{:S(2)}) collective-permute-start(f32[3,1,16,256]{3,2,1,0:T(8,128)S(1)} %get-tuple-element.59), channel_id=1, source_target_pairs={{4,0},{8,4},{12,8},{16,12},{20,16},{24,20},{28,24},{32,28},{36,32}... | collective-permute-start | bytes 147464 | tf_op jit(solution)/shard_map/ppermute | solution.py:25
  76.2 5.3 %collective-permute-start.2 = (f32[3,1,16,256]{3,2,1,0:T(8,128)S(1)}, f32[3,1,16,256]{3,2,1,0:T(8,128)S(1)}, u32[]{:S(2)}, u32[]{:S(2)}) collective-permute-start(f32[3,1,16,256]{3,2,1,0:T(8,128)S(1)} %get-tuple-element.58), channel_id=1, source_target_pairs={{0,4},{4,8},{8,12},{12,16},{16,20},{20,24},{24,28},{28,32},{32,36}... | collective-permute-start | bytes 147464 | tf_op jit(solution)/shard_map/ppermute | solution.py:22
  84.8 8.8 %collective-permute-start.5 = (f32[3,1,16,256]{3,2,1,0:T(8,128)S(1)}, f32[3,1,16,256]{3,2,1,0:T(8,128)S(1)}, u32[]{:S(2)}, u32[]{:S(2)}) collective-permute-start(f32[3,1,16,256]{3,2,1,0:T(8,128)S(1)} %get-tuple-element.57), channel_id=1, source_target_pairs={{4,0},{8,4},{12,8},{16,12},{20,16},{24,20},{28,24},{32,28},{36,32}... | collective-permute-start | bytes 147464 | tf_op jit(solution)/shard_map/ppermute | solution.py:25
  86.1 7.9 %collective-permute-start.4 = (f32[3,1,16,256]{3,2,1,0:T(8,128)S(1)}, f32[3,1,16,256]{3,2,1,0:T(8,128)S(1)}, u32[]{:S(2)}, u32[]{:S(2)}) collective-permute-start(f32[3,1,16,256]{3,2,1,0:T(8,128)S(1)} %get-tuple-element.56), channel_id=1, source_target_pairs={{0,4},{4,8},{8,12},{12,16},{16,20},{20,24},{24,28},{28,32},{32,36}... | collective-permute-start | bytes 147464 | tf_op jit(solution)/shard_map/ppermute | solution.py:22
  97.4 8.9 %collective-permute-start.7 = (f32[3,1,16,256]{3,2,1,0:T(8,128)S(1)}, f32[3,1,16,256]{3,2,1,0:T(8,128)S(1)}, u32[]{:S(2)}, u32[]{:S(2)}) collective-permute-start(f32[3,1,16,256]{3,2,1,0:T(8,128)S(1)} %get-tuple-element.55), channel_id=1, source_target_pairs={{4,0},{8,4},{12,8},{16,12},{20,16},{24,20},{28,24},{32,28},{36,32}... | collective-permute-start | bytes 147464 | tf_op jit(solution)/shard_map/ppermute | solution.py:25
  98.7 7.9 %collective-permute-start.6 = (f32[3,1,16,256]{3,2,1,0:T(8,128)S(1)}, f32[3,1,16,256]{3,2,1,0:T(8,128)S(1)}, u32[]{:S(2)}, u32[]{:S(2)}) collective-permute-start(f32[3,1,16,256]{3,2,1,0:T(8,128)S(1)} %get-tuple-element.54), channel_id=1, source_target_pairs={{0,4},{4,8},{8,12},{12,16},{16,20},{20,24},{24,28},{28,32},{32,36}... | collective-permute-start | bytes 147464 | tf_op jit(solution)/shard_map/ppermute | solution.py:22
  233.0 47.7 %all-to-all-start = ((f32[3,64,256]{2,0,1:T(4,128)}), f32[3,64,256]{2,0,1:T(4,128)S(1)}, u32[]{:S(2)}, u32[]{:S(2)}) async-start(f32[3,64,256]{2,0,1:T(4,128)} %multiply_bitcast_fusion), calls=%async_computation | async-start | bytes 524288 | tf_op jit(solution)/shard_map/all_to_all | solution.py:164
  263.9 260.2 %all-reduce.11.cloned.1.call-start = ((), (), s32[]{:S(2)}) async-start(), calls=%async_computation.1 | async-start | bytes 2097152 | tf_op jit(solution)/shard_map/psum | solution.py:176
  375.3 5.4 %collective-permute-start.11 = (f32[3,1,8,128]{3,2,1,0:T(8,128)S(1)}, f32[3,1,8,128]{3,2,1,0:T(8,128)S(1)}, u32[]{:S(2)}, u32[]{:S(2)}) collective-permute-start(f32[3,1,8,128]{3,2,1,0:T(8,128)S(1)} %get-tuple-element.99), channel_id=1, source_target_pairs={{4,0},{8,4},{12,8},{16,12},{20,16},{24,20},{28,24},{32,28},{36,32}... | collective-permute-start | bytes 36872 | tf_op jit(solution)/shard_map/ppermute | solution.py:25
  376.6 4.8 collective-permute-start.10
  382.5 5.6 %collective-permute-start.13 = (f32[3,1,8,128]{3,2,1,0:T(8,128)S(1)}, f32[3,1,8,128]{3,2,1,0:T(8,128)S(1)}, u32[]{:S(2)}, u32[]{:S(2)}) collective-permute-start(f32[3,1,8,128]{3,2,1,0:T(8,128)S(1)} %get-tuple-element.97), channel_id=1, source_target_pairs={{4,0},{8,4},{12,8},{16,12},{20,16},{24,20},{28,24},{32,28},{36,32}... | collective-permute-start | bytes 36872 | tf_op jit(solution)/shard_map/ppermute | solution.py:25
  383.8 5.1 collective-permute-start.12
  389.6 6.2 %collective-permute-start.15 = (f32[3,1,8,128]{3,2,1,0:T(8,128)S(1)}, f32[3,1,8,128]{3,2,1,0:T(8,128)S(1)}, u32[]{:S(2)}, u32[]{:S(2)}) collective-permute-start(f32[3,1,8,128]{3,2,1,0:T(8,128)S(1)} %get-tuple-element.95), channel_id=1, source_target_pairs={{4,0},{8,4},{12,8},{16,12},{20,16},{24,20},{28,24},{32,28},{36,32}... | collective-permute-start | bytes 36872 | tf_op jit(solution)/shard_map/ppermute | solution.py:25
  390.9 5.1 collective-permute-start.14
  404.8 9.0 %collective-permute-start.17 = (f32[3,1,16,256]{3,2,1,0:T(8,128)}, f32[3,1,16,256]{3,2,1,0:T(8,128)}, u32[]{:S(2)}, u32[]{:S(2)}) collective-permute-start(f32[3,1,16,256]{3,2,1,0:T(8,128)} %get-tuple-element.53), channel_id=1, source_target_pairs={{4,0},{8,4},{12,8},{16,12},{20,16},{24,20},{28,24},{32,28},{36,32}... | collective-permute-start | bytes 147464 | tf_op jit(solution)/shard_map/ppermute | solution.py:25
  406.1 7.7 %collective-permute-start.16 = (f32[3,1,16,256]{3,2,1,0:T(8,128)}, f32[3,1,16,256]{3,2,1,0:T(8,128)}, u32[]{:S(2)}, u32[]{:S(2)}) collective-permute-start(f32[3,1,16,256]{3,2,1,0:T(8,128)} %get-tuple-element.52), channel_id=1, source_target_pairs={{0,4},{4,8},{8,12},{12,16},{16,20},{20,24},{24,28},{28,32},{32,36}... | collective-permute-start | bytes 147464 | tf_op jit(solution)/shard_map/ppermute | solution.py:22
  (83 other events, 832.2 us)
Sparse Core Ops, SparseCore 0:
  423.0 101.0 all-reduce.10
where the time goes:
time: 535 us; the launch traced here: 534 us
  local copies, waits for them, and re-layouts  170 us (32%)
  other arithmetic  156 us (29%)
  waiting for transfers between devices  104 us (19%)
  starting transfers between devices  87.7 us (16%)
  between operations  16 us (3%)
    psum x1, waiting for transfers between devices, body(): total_sum = lax.psum(energy, 'load')  101 us
    scatter-add x1, other arithmetic, body(): coarse_source.reshape(3, -1).at[:, face_dst[0]].add(arrived)  88.6 us
    gather x2, local copies, waits for them, and re-layouts, body(): picked = residual.reshape(3, -1)[:, face_src[0]] * live_mask[None]  65.9 us
    ppermute x9, starting transfers between devices, extended(): lax.ppermute(lax.slice_in_dim(block, block.shape[dim] - width, None, axis...  45.2 us
    another operation x4, local copies, waits for them, and re-layouts, operate(): return jnp.stack(pieces)  37.8 us
    all_to_all x1, starting transfers between devices, body(): lax.all_to_all(picked, 'space', split_axis=1, concat_axis=1, tiled=True)  30.9 us
    squeeze x1, local copies, waits for them, and re-layouts, body(): source = load_force[0]  26.5 us
    reduce_sum x2, other arithmetic, coarsen(): grid_field.reshape(comps, size_x // 2, 2, size_y // 2, 2, size_z // 2, 2)  20.2 us
  transfers between devices with their start and end apart: 20, of which 7 were waited for; matrix products, arithmetic and copies ran while one was open for 14% of the time, Pallas kernels for 0%

commit v1 on v0

--- a/solution.py
+++ b/solution.py
@@ -173,7 +173,7 @@
     outputs = [displaced]
     rows_part = NY // lax.axis_size("load")
     start_row = lax.axis_index("load") * rows_part
-    total_sum = lax.psum(energy, "load")
+    total_sum = jnp.sum(lax.all_gather(energy, axis_name="load"), axis=0)
     energy_part = lax.dynamic_slice_in_dim(total_sum, start_row, rows_part, 1)
     own_part = lax.dynamic_slice_in_dim(own_cells, start_row, rows_part, 1)[None]
     moduli = jnp.array(MODULI, jnp.float32)[:, None, None, None]

time: 535 us -> 460 us (0.86)
  the two profiles are of different devices: /device:TPU:1 before, /device:TPU:7 now
where the time goes in v1:
time: 460 us; the launch traced here: 459 us
  local copies, waits for them, and re-layouts  166 us (36%)
  other arithmetic  156 us (34%)
  starting transfers between devices  71.6 us (16%)
  waiting for transfers between devices  41.1 us (9%)
  blocking collectives  22.1 us (5%)
    scatter-add x1, other arithmetic, body(): coarse_source.reshape(3, -1).at[:, face_dst[0]].add(arrived)  88.6 us
    gather x2, local copies, waits for them, and re-layouts, body(): picked = residual.reshape(3, -1)[:, face_src[0]] * live_mask[None]  65.6 us
    ppermute x9, starting transfers between devices, extended(): lax.ppermute(lax.slice_in_dim(block, 0, width, axis=dim), axis, backward)  42.2 us
    ppermute x9, waiting for transfers between devices, extended(): lax.ppermute(lax.slice_in_dim(block, block.shape[dim] - width, None, axis...  41.1 us
    another operation x4, local copies, waits for them, and re-layouts, operate(): return jnp.stack(pieces)  37.7 us
    squeeze x1, local copies, waits for them, and re-layouts, body(): source = load_force[0]  26.5 us
    ppermute x9, starting transfers between devices, extended(): lax.ppermute(lax.slice_in_dim(block, block.shape[dim] - width, None, axis...  24.7 us
    all_gather x1, blocking collectives, body(): total_sum = jnp.sum(lax.all_gather(energy, axis_name='load'), axis=0)  22.1 us
  transfers between devices with their start and end apart: 19, of which 7 were waited for; matrix products, arithmetic and copies ran while one was open for 16% of the time, Pallas kernels for 0%

profile of v1, /device:TPU:7, one launch (start us, length us, event | category | flops | bytes accessed | tf_op | source)
XLA Modules:
  0.0 459.3 jit_solution(15434045661951338468)
XLA Ops:
  2.6 9.0 %collective-permute-start.1 = (f32[1,1,16,256]{3,2,1,0:T(8,128)S(1)}, f32[1,1,16,256]{3,2,1,0:T(8,128)S(1)}, u32[]{:S(2)}, u32[]{:S(2)}) collective-permute-start(f32[1,1,16,256]{3,2,1,0:T(8,128)S(1)} %get-tuple-element.69), channel_id=1, source_target_pairs={{4,0},{8,4},{12,8},{16,12},{20,16},{24,20},{28,24},{32,28},{36,32}... | collective-permute-start | bytes 49160 | tf_op jit(solution)/shard_map/ppermute | solution.py:25
  14.6 9.8 %reshape_broadcast_in_dim.3 = f32[4,2,8,2,128,2]{5,4,3,2,1,0:T(8,128)} reshape(f32[8,16,256]{2,1,0:T(8,128)S(1)} %broadcast_multiply_fusion.1) | data formatting | bytes 262144 | tf_op jit(solution)/shard_map/reshape;broadcast_in_dim | solution.py:123
  24.3 4.1 reduce_sum.47
  28.4 8.2 %collective-permute-start.9 = (f32[1,1,8,128]{3,2,1,0:T(8,128)S(1)}, f32[1,1,8,128]{3,2,1,0:T(8,128)S(1)}, u32[]{:S(2)}, u32[]{:S(2)}) collective-permute-start(f32[1,1,8,128]{3,2,1,0:T(8,128)S(1)} %get-tuple-element.103), channel_id=1, source_target_pairs={{4,0},{8,4},{12,8},{16,12},{20,16},{24,20},{28,24},{32,28},{36,32}... | collective-permute-start | bytes 12296 | tf_op jit(solution)/shard_map/ppermute | solution.py:25
  40.0 26.5 %squeeze.11 = f32[3,4,2,8,2,128,2]{6,5,4,3,2,1,0:T(8,128)} reshape(f32[1,3,8,16,256]{4,3,2,1,0:T(8,128)S(1)} %copy-done) | data formatting | bytes 786432 | tf_op jit(solution)/shard_map/squeeze | solution.py:159
  66.5 8.6 %copy.310 = f32[1,3,8,16,256]{1,4,3,2,0:T(8,128)} copy(f32[1,3,8,16,256]{4,3,2,1,0:T(8,128)S(1)} %copy-done) | data formatting | bytes 786432 | tf_op args[0]
  77.5 8.2 %collective-permute-start.3 = (f32[3,1,16,256]{3,2,1,0:T(8,128)S(1)}, f32[3,1,16,256]{3,2,1,0:T(8,128)S(1)}, u32[]{:S(2)}, u32[]{:S(2)}) collective-permute-start(f32[3,1,16,256]{3,2,1,0:T(8,128)S(1)} %get-tuple-element.59), channel_id=1, source_target_pairs={{4,0},{8,4},{12,8},{16,12},{20,16},{24,20},{28,24},{32,28},{36,32}... | collective-permute-start | bytes 147464 | tf_op jit(solution)/shard_map/ppermute | solution.py:25
  87.9 7.4 %collective-permute-done.2 = f32[3,1,16,256]{3,2,1,0:T(8,128)S(1)} collective-permute-done((f32[3,1,16,256]{3,2,1,0:T(8,128)S(1)}, f32[3,1,16,256]{3,2,1,0:T(8,128)S(1)}, u32[]{:S(2)}, u32[]{:S(2)}) %collective-permute-start.2) | collective-permute-done | bytes 49184 | tf_op jit(solution)/shard_map/ppermute | solution.py:22
  100.5 3.4 collective-permute-start.4
  104.7 5.5 %collective-permute-done.4 = f32[3,1,16,256]{3,2,1,0:T(8,128)S(1)} collective-permute-done((f32[3,1,16,256]{3,2,1,0:T(8,128)S(1)}, f32[3,1,16,256]{3,2,1,0:T(8,128)S(1)}, u32[]{:S(2)}, u32[]{:S(2)}) %collective-permute-start.4) | collective-permute-done | bytes 49184 | tf_op jit(solution)/shard_map/ppermute | solution.py:22
  115.6 3.5 collective-permute-start.6
  119.9 5.3 %collective-permute-done.6 = f32[3,1,16,256]{3,2,1,0:T(8,128)S(1)} collective-permute-done((f32[3,1,16,256]{3,2,1,0:T(8,128)S(1)}, f32[3,1,16,256]{3,2,1,0:T(8,128)S(1)}, u32[]{:S(2)}, u32[]{:S(2)}) %collective-permute-start.6) | collective-permute-done | bytes 49184 | tf_op jit(solution)/shard_map/ppermute | solution.py:22
  128.6 9.7 %stack.91 = f32[1,4,2,8,2,128,2]{6,5,4,3,2,1,0:T(8,128)} reshape(f32[1,8,16,256]{3,2,1,0:T(8,128)S(1)} %fusion.270) | data formatting | bytes 262144 | tf_op jit(solution)/shard_map/stack | solution.py:87
  138.3 9.7 %stack.90 = f32[1,4,2,8,2,128,2]{6,5,4,3,2,1,0:T(8,128)} reshape(f32[1,8,16,256]{3,2,1,0:T(8,128)S(1)} %get-tuple-element.23) | data formatting | bytes 262144 | tf_op jit(solution)/shard_map/stack | solution.py:87
  148.0 9.7 %stack.89 = f32[1,4,2,8,2,128,2]{6,5,4,3,2,1,0:T(8,128)} reshape(f32[1,8,16,256]{3,2,1,0:T(8,128)S(1)} %get-tuple-element.22) | data formatting | bytes 262144 | tf_op jit(solution)/shard_map/stack | solution.py:87
  158.5 8.5 %copy.311 = f32[3,32768]{0,1:T(8,128)} copy(f32[3,32768]{1,0:T(4,128)S(1)} %pad_maximum_fusion) | data formatting | bytes 786432 | tf_op jit(solution)/shard_map/stack | solution.py:87
  167.1 17.8 %bitcast_subtract_fusion = f32[3,32768]{0,1:T(8,128)} fusion(f32[3,32768]{0,1:T(8,128)} %copy.311, f32[1,3,8,16,256]{1,4,3,2,0:T(8,128)} %copy.310), kind=kLoop, calls=%fused_computation.4 | loop fusion | flops 98304 | bytes 1179648 | tf_op jit(solution)/shard_map/sub | solution.py:161
  184.9 60.2 %gather_fusion = f32[16384,3]{1,0:T(8,128)} fusion(f32[3,32768]{0,1:T(8,128)} %bitcast_subtract_fusion, s32[16384]{0:T(1024)S(1)} %copy-done.77), kind=kCustom, calls=%fused_computation | custom fusion | bytes 458752 | tf_op jit(solution)/shard_map/gather | solution.py:163
  245.1 5.4 %copy.312 = f32[64,256,3]{1,2,0:T(4,128)S(1)} copy(f32[64,256,3]{2,1,0:T(8,128)} %bitcast.289) | data formatting | bytes 393216 | tf_op jit(solution)/shard_map/gather | solution.py:163
  251.3 4.7 %all-to-all-start = ((f32[3,64,256]{2,0,1:T(4,128)}), f32[3,64,256]{2,0,1:T(4,128)S(1)}, u32[]{:S(2)}, u32[]{:S(2)}) async-start(f32[3,64,256]{2,0,1:T(4,128)} %multiply_bitcast_fusion), calls=%async_computation | async-start | bytes 524288 | tf_op jit(solution)/shard_map/all_to_all | solution.py:164
  256.0 16.1 %fusion = f32[3,4,8,128]{3,2,1,0:T(8,128)S(1)} fusion(f32[3,4,2,8,2,128,2]{6,5,4,3,2,1,0:T(8,128)} %squeeze.11, f32[1,4,2,8,2,128,2]{6,5,4,3,2,1,0:T(8,128)} %stack.91, f32[1,4,2,8,2,128,2]{6,5,4,3,2,1,0:T(8,128)} %stack.90, f32[1,4,2,8,2,128,2]{6,5,4,3,2,1,0:T(8,128)} %stack.89), kind=kLoop, calls=%fused_computation.3 | loop fusion | flops 380928 | bytes 835584 | tf_op jit(solution)/shard_map/reduce_sum | solution.py:123
  272.8 5.1 %copy.313 = f32[16384,3]{1,0:T(8,128)} copy(f32[16384,3]{0,1:T(4,128)S(1)} %bitcast.304) | data formatting | bytes 393216 | tf_op jit(solution)/shard_map/all_to_all | solution.py:164
  277.9 88.6 %scatter_fusion = f32[3,4096]{0,1:T(8,128)S(1)} fusion(f32[3,4096]{0,1:T(8,128)S(1)} %bitcast.287, s32[16384]{0:T(1024)S(1)} %bitcast.314, f32[16384,3]{1,0:T(8,128)} %copy.313), kind=kCustom, calls=%fused_computation.1 | custom fusion | flops 49152 | bytes 655360 | tf_op jit(solution)/shard_map/scatter-add | solution.py:166
  367.4 7.3 %collective-permute-start.11 = (f32[3,1,8,128]{3,2,1,0:T(8,128)S(1)}, f32[3,1,8,128]{3,2,1,0:T(8,128)S(1)}, u32[]{:S(2)}, u32[]{:S(2)}) collective-permute-start(f32[3,1,8,128]{3,2,1,0:T(8,128)S(1)} %get-tuple-element.99), channel_id=1, source_target_pairs={{4,0},{8,4},{12,8},{16,12},{20,16},{24,20},{28,24},{32,28},{36,32}... | collective-permute-start | bytes 36872 | tf_op jit(solution)/shard_map/ppermute | solution.py:25
  376.7 7.2 %collective-permute-done.10 = f32[3,1,8,128]{3,2,1,0:T(8,128)S(1)} collective-permute-done((f32[3,1,8,128]{3,2,1,0:T(8,128)S(1)}, f32[3,1,8,128]{3,2,1,0:T(8,128)S(1)}, u32[]{:S(2)}, u32[]{:S(2)}) %collective-permute-start.10) | collective-permute-done | bytes 12320 | tf_op jit(solution)/shard_map/ppermute | solution.py:22
  386.9 3.4 collective-permute-start.12
  390.4 5.8 %collective-permute-done.12 = f32[3,1,8,128]{3,2,1,0:T(8,128)S(1)} collective-permute-done((f32[3,1,8,128]{3,2,1,0:T(8,128)S(1)}, f32[3,1,8,128]{3,2,1,0:T(8,128)S(1)}, u32[]{:S(2)}, u32[]{:S(2)}) %collective-permute-start.12) | collective-permute-done | bytes 12320 | tf_op jit(solution)/shard_map/ppermute | solution.py:22
  398.8 3.4 collective-permute-start.14
  402.8 5.3 %collective-permute-done.14 = f32[3,1,8,128]{3,2,1,0:T(8,128)S(1)} collective-permute-done((f32[3,1,8,128]{3,2,1,0:T(8,128)S(1)}, f32[3,1,8,128]{3,2,1,0:T(8,128)S(1)}, u32[]{:S(2)}, u32[]{:S(2)}) %collective-permute-start.14) | collective-permute-done | bytes 12320 | tf_op jit(solution)/shard_map/ppermute | solution.py:22
  418.9 3.4 collective-permute-start.16
  424.2 4.6 %collective-permute-done.16 = f32[3,1,16,256]{3,2,1,0:T(8,128)} collective-permute-done((f32[3,1,16,256]{3,2,1,0:T(8,128)}, f32[3,1,16,256]{3,2,1,0:T(8,128)}, u32[]{:S(2)}, u32[]{:S(2)}) %collective-permute-start.16) | collective-permute-done | bytes 49184 | tf_op jit(solution)/shard_map/ppermute | solution.py:22
  436.4 22.1 %all-gather = f32[32,16,256]{2,1,0:T(8,128)S(1)} all-gather(f32[8,16,256]{2,1,0:T(8,128)S(1)} %get-tuple-element.12), channel_id=2, replica_groups=mesh['space'=64,'load'=4] {'load'}, dimensions={0}, use_global_device_ids=true | all-gather | bytes 655360 | tf_op jit(solution)/shard_map/all_gather | solution.py:176
  (298 shorter events, 59.3 us)
Async XLA Ops:
  1.6 96.2 %copy-start.79 = (f32[16]{0:T(128)}, f32[16]{0:T(128)S(1)}, u32[]{:S(2)}) copy-start(f32[16]{0:T(128)S(1)} %broadcast_in_dim.30) | copy-start | bytes 196
  2.6 73.2 %collective-permute-start.1 = (f32[1,1,16,256]{3,2,1,0:T(8,128)S(1)}, f32[1,1,16,256]{3,2,1,0:T(8,128)S(1)}, u32[]{:S(2)}, u32[]{:S(2)}) collective-permute-start(f32[1,1,16,256]{3,2,1,0:T(8,128)S(1)} %get-tuple-element.69), channel_id=1, source_target_pairs={{4,0},{8,4},{12,8},{16,12},{20,16},{24,20},{28,24},{32,28},{36,32}... | collective-permute-start | bytes 49160 | tf_op jit(solution)/shard_map/ppermute | solution.py:25
  11.6 64.2 %collective-permute-start = (f32[1,1,16,256]{3,2,1,0:T(8,128)S(1)}, f32[1,1,16,256]{3,2,1,0:T(8,128)S(1)}, u32[]{:S(2)}, u32[]{:S(2)}) collective-permute-start(f32[1,1,16,256]{3,2,1,0:T(8,128)S(1)} %get-tuple-element.68), channel_id=1, source_target_pairs={{0,4},{4,8},{8,12},{12,16},{16,20},{20,24},{24,28},{28,32},{32,36}... | collective-permute-start | bytes 49160 | tf_op jit(solution)/shard_map/ppermute | solution.py:22
  28.4 47.3 %collective-permute-start.9 = (f32[1,1,8,128]{3,2,1,0:T(8,128)S(1)}, f32[1,1,8,128]{3,2,1,0:T(8,128)S(1)}, u32[]{:S(2)}, u32[]{:S(2)}) collective-permute-start(f32[1,1,8,128]{3,2,1,0:T(8,128)S(1)} %get-tuple-element.103), channel_id=1, source_target_pairs={{4,0},{8,4},{12,8},{16,12},{20,16},{24,20},{28,24},{32,28},{36,32}... | collective-permute-start | bytes 12296 | tf_op jit(solution)/shard_map/ppermute | solution.py:25
  36.6 39.1 %collective-permute-start.8 = (f32[1,1,8,128]{3,2,1,0:T(8,128)S(1)}, f32[1,1,8,128]{3,2,1,0:T(8,128)S(1)}, u32[]{:S(2)}, u32[]{:S(2)}) collective-permute-start(f32[1,1,8,128]{3,2,1,0:T(8,128)S(1)} %get-tuple-element.102), channel_id=1, source_target_pairs={{0,4},{4,8},{8,12},{12,16},{16,20},{20,24},{24,28},{28,32},{32,36}... | collective-permute-start | bytes 12296 | tf_op jit(solution)/shard_map/ppermute | solution.py:22
  76.6 49.0 %copy-start.15 = (f32[8,16,256]{2,1,0:T(8,128)}, f32[8,16,256]{2,1,0:T(8,128)S(1)}, u32[]{:S(2)}) copy-start(f32[8,16,256]{2,1,0:T(8,128)S(1)} %get-tuple-element.28) | copy-start | bytes 393220
  76.6 49.0 %copy-start.17 = (f32[8,16,256]{2,1,0:T(8,128)}, f32[8,16,256]{2,1,0:T(8,128)S(1)}, u32[]{:S(2)}) copy-start(f32[8,16,256]{2,1,0:T(8,128)S(1)} %get-tuple-element.29) | copy-start | bytes 393220
  76.6 49.0 %copy-start.19 = (f32[8,16,256]{2,1,0:T(8,128)}, f32[8,16,256]{2,1,0:T(8,128)S(1)}, u32[]{:S(2)}) copy-start(f32[8,16,256]{2,1,0:T(8,128)S(1)} %get-tuple-element.30) | copy-start | bytes 393220
  76.6 49.0 %copy-start.21 = (f32[8,16,256]{2,1,0:T(8,128)}, f32[8,16,256]{2,1,0:T(8,128)S(1)}, u32[]{:S(2)}) copy-start(f32[8,16,256]{2,1,0:T(8,128)S(1)} %get-tuple-element.31) | copy-start | bytes 393220
  76.6 49.0 %copy-start.23 = (f32[8,16,256]{2,1,0:T(8,128)}, f32[8,16,256]{2,1,0:T(8,128)S(1)}, u32[]{:S(2)}) copy-start(f32[8,16,256]{2,1,0:T(8,128)S(1)} %get-tuple-element.32) | copy-start | bytes 393220
  76.7 49.0 %copy-start.25 = (f32[8,16,256]{2,1,0:T(8,128)}, f32[8,16,256]{2,1,0:T(8,128)S(1)}, u32[]{:S(2)}) copy-start(f32[8,16,256]{2,1,0:T(8,128)S(1)} %get-tuple-element.33) | copy-start | bytes 393220
  76.7 49.0 %copy-start.27 = (f32[8,16,256]{2,1,0:T(8,128)}, f32[8,16,256]{2,1,0:T(8,128)S(1)}, u32[]{:S(2)}) copy-start(f32[8,16,256]{2,1,0:T(8,128)S(1)} %get-tuple-element.34) | copy-start | bytes 393220
  76.7 49.0 %copy-start.29 = (f32[8,16,256]{2,1,0:T(8,128)}, f32[8,16,256]{2,1,0:T(8,128)S(1)}, u32[]{:S(2)}) copy-start(f32[8,16,256]{2,1,0:T(8,128)S(1)} %get-tuple-element.35) | copy-start | bytes 393220
  76.7 49.0 %copy-start.31 = (f32[8,16,256]{2,1,0:T(8,128)}, f32[8,16,256]{2,1,0:T(8,128)S(1)}, u32[]{:S(2)}) copy-start(f32[8,16,256]{2,1,0:T(8,128)S(1)} %get-tuple-element.36) | copy-start | bytes 393220
  76.7 49.0 %copy-start.33 = (f32[8,16,256]{2,1,0:T(8,128)}, f32[8,16,256]{2,1,0:T(8,128)S(1)}, u32[]{:S(2)}) copy-start(f32[8,16,256]{2,1,0:T(8,128)S(1)} %get-tuple-element.37) | copy-start | bytes 393220
  76.7 49.0 %copy-start.34 = (f32[8,16,256]{2,1,0:T(8,128)}, f32[8,16,256]{2,1,0:T(8,128)S(1)}, u32[]{:S(2)}) copy-start(f32[8,16,256]{2,1,0:T(8,128)S(1)} %get-tuple-element.38) | copy-start | bytes 393220
  76.7 49.0 %copy-start.35 = (f32[8,16,256]{2,1,0:T(8,128)}, f32[8,16,256]{2,1,0:T(8,128)S(1)}, u32[]{:S(2)}) copy-start(f32[8,16,256]{2,1,0:T(8,128)S(1)} %get-tuple-element.39) | copy-start | bytes 393220
  77.5 10.4 %collective-permute-start.3 = (f32[3,1,16,256]{3,2,1,0:T(8,128)S(1)}, f32[3,1,16,256]{3,2,1,0:T(8,128)S(1)}, u32[]{:S(2)}, u32[]{:S(2)}) collective-permute-start(f32[3,1,16,256]{3,2,1,0:T(8,128)S(1)} %get-tuple-element.59), channel_id=1, source_target_pairs={{4,0},{8,4},{12,8},{16,12},{20,16},{24,20},{28,24},{32,28},{36,32}... | collective-permute-start | bytes 147464 | tf_op jit(solution)/shard_map/ppermute | solution.py:25
  85.6 9.7 %collective-permute-start.2 = (f32[3,1,16,256]{3,2,1,0:T(8,128)S(1)}, f32[3,1,16,256]{3,2,1,0:T(8,128)S(1)}, u32[]{:S(2)}, u32[]{:S(2)}) collective-permute-start(f32[3,1,16,256]{3,2,1,0:T(8,128)S(1)} %get-tuple-element.58), channel_id=1, source_target_pairs={{0,4},{4,8},{8,12},{12,16},{16,20},{20,24},{24,28},{28,32},{32,36}... | collective-permute-start | bytes 147464 | tf_op jit(solution)/shard_map/ppermute | solution.py:22
  98.6 6.1 %collective-permute-start.5 = (f32[3,1,16,256]{3,2,1,0:T(8,128)S(1)}, f32[3,1,16,256]{3,2,1,0:T(8,128)S(1)}, u32[]{:S(2)}, u32[]{:S(2)}) collective-permute-start(f32[3,1,16,256]{3,2,1,0:T(8,128)S(1)} %get-tuple-element.57), channel_id=1, source_target_pairs={{4,0},{8,4},{12,8},{16,12},{20,16},{24,20},{28,24},{32,28},{36,32}... | collective-permute-start | bytes 147464 | tf_op jit(solution)/shard_map/ppermute | solution.py:25
  100.5 9.7 %collective-permute-start.4 = (f32[3,1,16,256]{3,2,1,0:T(8,128)S(1)}, f32[3,1,16,256]{3,2,1,0:T(8,128)S(1)}, u32[]{:S(2)}, u32[]{:S(2)}) collective-permute-start(f32[3,1,16,256]{3,2,1,0:T(8,128)S(1)} %get-tuple-element.56), channel_id=1, source_target_pairs={{0,4},{4,8},{8,12},{12,16},{16,20},{20,24},{24,28},{28,32},{32,36}... | collective-permute-start | bytes 147464 | tf_op jit(solution)/shard_map/ppermute | solution.py:22
  113.7 6.3 %collective-permute-start.7 = (f32[3,1,16,256]{3,2,1,0:T(8,128)S(1)}, f32[3,1,16,256]{3,2,1,0:T(8,128)S(1)}, u32[]{:S(2)}, u32[]{:S(2)}) collective-permute-start(f32[3,1,16,256]{3,2,1,0:T(8,128)S(1)} %get-tuple-element.55), channel_id=1, source_target_pairs={{4,0},{8,4},{12,8},{16,12},{20,16},{24,20},{28,24},{32,28},{36,32}... | collective-permute-start | bytes 147464 | tf_op jit(solution)/shard_map/ppermute | solution.py:25
  115.6 9.6 %collective-permute-start.6 = (f32[3,1,16,256]{3,2,1,0:T(8,128)S(1)}, f32[3,1,16,256]{3,2,1,0:T(8,128)S(1)}, u32[]{:S(2)}, u32[]{:S(2)}) collective-permute-start(f32[3,1,16,256]{3,2,1,0:T(8,128)S(1)} %get-tuple-element.54), channel_id=1, source_target_pairs={{0,4},{4,8},{8,12},{12,16},{16,20},{20,24},{24,28},{28,32},{32,36}... | collective-permute-start | bytes 147464 | tf_op jit(solution)/shard_map/ppermute | solution.py:22
  251.3 21.5 %all-to-all-start = ((f32[3,64,256]{2,0,1:T(4,128)}), f32[3,64,256]{2,0,1:T(4,128)S(1)}, u32[]{:S(2)}, u32[]{:S(2)}) async-start(f32[3,64,256]{2,0,1:T(4,128)} %multiply_bitcast_fusion), calls=%async_computation | async-start | bytes 524288 | tf_op jit(solution)/shard_map/all_to_all | solution.py:164
  367.4 9.3 %collective-permute-start.11 = (f32[3,1,8,128]{3,2,1,0:T(8,128)S(1)}, f32[3,1,8,128]{3,2,1,0:T(8,128)S(1)}, u32[]{:S(2)}, u32[]{:S(2)}) collective-permute-start(f32[3,1,8,128]{3,2,1,0:T(8,128)S(1)} %get-tuple-element.99), channel_id=1, source_target_pairs={{4,0},{8,4},{12,8},{16,12},{20,16},{24,20},{28,24},{32,28},{36,32}... | collective-permute-start | bytes 36872 | tf_op jit(solution)/shard_map/ppermute | solution.py:25
  374.7 9.2 %collective-permute-start.10 = (f32[3,1,8,128]{3,2,1,0:T(8,128)S(1)}, f32[3,1,8,128]{3,2,1,0:T(8,128)S(1)}, u32[]{:S(2)}, u32[]{:S(2)}) collective-permute-start(f32[3,1,8,128]{3,2,1,0:T(8,128)S(1)} %get-tuple-element.98), channel_id=1, source_target_pairs={{0,4},{4,8},{8,12},{12,16},{16,20},{20,24},{24,28},{28,32},{32,36}... | collective-permute-start | bytes 36872 | tf_op jit(solution)/shard_map/ppermute | solution.py:22
  385.0 5.4 %collective-permute-start.13 = (f32[3,1,8,128]{3,2,1,0:T(8,128)S(1)}, f32[3,1,8,128]{3,2,1,0:T(8,128)S(1)}, u32[]{:S(2)}, u32[]{:S(2)}) collective-permute-start(f32[3,1,8,128]{3,2,1,0:T(8,128)S(1)} %get-tuple-element.97), channel_id=1, source_target_pairs={{4,0},{8,4},{12,8},{16,12},{20,16},{24,20},{28,24},{32,28},{36,32}... | collective-permute-start | bytes 36872 | tf_op jit(solution)/shard_map/ppermute | solution.py:25
  386.9 9.2 %collective-permute-start.12 = (f32[3,1,8,128]{3,2,1,0:T(8,128)S(1)}, f32[3,1,8,128]{3,2,1,0:T(8,128)S(1)}, u32[]{:S(2)}, u32[]{:S(2)}) collective-permute-start(f32[3,1,8,128]{3,2,1,0:T(8,128)S(1)} %get-tuple-element.96), channel_id=1, source_target_pairs={{0,4},{4,8},{8,12},{12,16},{16,20},{20,24},{24,28},{28,32},{32,36}... | collective-permute-start | bytes 36872 | tf_op jit(solution)/shard_map/ppermute | solution.py:22
  396.9 5.9 %collective-permute-start.15 = (f32[3,1,8,128]{3,2,1,0:T(8,128)S(1)}, f32[3,1,8,128]{3,2,1,0:T(8,128)S(1)}, u32[]{:S(2)}, u32[]{:S(2)}) collective-permute-start(f32[3,1,8,128]{3,2,1,0:T(8,128)S(1)} %get-tuple-element.95), channel_id=1, source_target_pairs={{4,0},{8,4},{12,8},{16,12},{20,16},{24,20},{28,24},{32,28},{36,32}... | collective-permute-start | bytes 36872 | tf_op jit(solution)/shard_map/ppermute | solution.py:25
  398.8 9.3 %collective-permute-start.14 = (f32[3,1,8,128]{3,2,1,0:T(8,128)S(1)}, f32[3,1,8,128]{3,2,1,0:T(8,128)S(1)}, u32[]{:S(2)}, u32[]{:S(2)}) collective-permute-start(f32[3,1,8,128]{3,2,1,0:T(8,128)S(1)} %get-tuple-element.94), channel_id=1, source_target_pairs={{0,4},{4,8},{8,12},{12,16},{16,20},{20,24},{24,28},{28,32},{32,36}... | collective-permute-start | bytes 36872 | tf_op jit(solution)/shard_map/ppermute | solution.py:22
  417.0 7.3 %collective-permute-start.17 = (f32[3,1,16,256]{3,2,1,0:T(8,128)}, f32[3,1,16,256]{3,2,1,0:T(8,128)}, u32[]{:S(2)}, u32[]{:S(2)}) collective-permute-start(f32[3,1,16,256]{3,2,1,0:T(8,128)} %get-tuple-element.53), channel_id=1, source_target_pairs={{4,0},{8,4},{12,8},{16,12},{20,16},{24,20},{28,24},{32,28},{36,32}... | collective-permute-start | bytes 147464 | tf_op jit(solution)/shard_map/ppermute | solution.py:25
  418.9 10.0 %collective-permute-start.16 = (f32[3,1,16,256]{3,2,1,0:T(8,128)}, f32[3,1,16,256]{3,2,1,0:T(8,128)}, u32[]{:S(2)}, u32[]{:S(2)}) collective-permute-start(f32[3,1,16,256]{3,2,1,0:T(8,128)} %get-tuple-element.52), channel_id=1, source_target_pairs={{0,4},{4,8},{8,12},{12,16},{16,20},{20,24},{24,28},{28,32},{32,36}... | collective-permute-start | bytes 147464 | tf_op jit(solution)/shard_map/ppermute | solution.py:22
  (82 other events, 1272.4 us)
